TPU v7x, 256 devices: a whole 4x4x8 slice. The times are simulated.
256 devices in a mesh: grp: 8 (over z_hi, y), slab: 32 (over x, z_lo, core).
Axes of the slice: x: 4, y: 4, z: 8 (z_hi: 2, z_lo: 4; z = z_hi * 4 + z_lo), core: 2. Of those that a mesh axis runs over, the one named last changes fastest.
Arguments:
- orbital_alpha: bfloat16 [8, 1536, 2560], P('grp', 'slab'), may hold values from -0.4375 to 0.4375
- orbital_beta: bfloat16 [8, 1536, 2560], P('grp', 'slab'), may hold values from -0.4375 to 0.4375
- occ_alpha: float32 [8], replicated, may hold values from -2 to -0.3
- occ_beta: float32 [8], replicated, may hold values from -2 to -0.3
- virt_alpha: float32 [1536], replicated, may hold values from 0.1 to 3
- virt_beta: float32 [1536], replicated, may hold values from 0.1 to 3
Outputs:
- grad_alpha: float32 [8, 1536, 2560], P('grp', 'slab')
- grad_beta: float32 [8, 1536, 2560], P('grp', 'slab')
All inputs are finite; a program needn't handle non-finite values.
Results may differ from a plain program's by a relative error of at most 0.0013.
Values may be sent and summed in bfloat16 or wider, within the bound.
A program may use at most 128 MiB of HBM per device.

v0:
```python
import jax
import jax.numpy as jnp
from jax import lax
from jax.sharding import PartitionSpec as P


def passed_along(value, axis, by):
    length = lax.axis_size(axis)
    return lax.ppermute(value, axis, [(i, (i + by) % length) for i in range(length)])


def body(orbital_alpha, orbital_beta, occ_alpha, occ_beta, virt_alpha, virt_beta):
    groups = lax.axis_size("grp")
    grp_index = lax.axis_index("grp")
    slab_index = lax.axis_index("slab")
    occ_count, virt_width, aux_width = orbital_alpha.shape
    beta_count = orbital_beta.shape[0]
    virt_total = virt_width * lax.axis_size("slab")
    own_virt = lax.dynamic_slice_in_dim(virt_beta, slab_index * virt_width, virt_width, 0)
    own_occ = lax.dynamic_slice_in_dim(occ_alpha, grp_index * occ_count, occ_count, 0)
    piece = lax.all_gather(orbital_alpha, "slab", axis=1, tiled=True)
    block_rows = jnp.einsum(
        "iaq,jbq->aijb", piece, orbital_beta, preferred_element_type=jnp.float32
    )
    panel_beta = orbital_beta
    amps_list = []
    panel_list = []
    beta_accum = jnp.zeros((groups * beta_count, virt_width, aux_width), jnp.float32)
    for section_index in range(groups):
        source = (grp_index - section_index) % groups
        if section_index == 0:
            integrals = block_rows
        else:
            integrals = jnp.einsum(
                "iaq,jbq->aijb", piece, panel_beta, preferred_element_type=jnp.float32
            )
        occ_source = lax.dynamic_slice_in_dim(occ_beta, source * beta_count, beta_count, 0)
        denominator = (
            virt_alpha[:, None, None, None]
            + own_virt[None, None, None, :]
            - own_occ[None, :, None, None]
            - occ_source[None, None, :, None]
        )
        amplitudes = (-integrals / denominator).astype(jnp.bfloat16)
        beta_term = jnp.einsum(
            "aijb,iaq->jbq", amplitudes, piece, preferred_element_type=jnp.float32
        )
        amps_list.append(amplitudes.reshape(virt_total * occ_count, beta_count * virt_width))
        panel_list.append(panel_beta.reshape(beta_count * virt_width, aux_width))
        beta_accum = lax.dynamic_update_slice_in_dim(beta_accum, beta_term, source * beta_count, 0)
        if section_index + 1 < groups:
            panel_beta = passed_along(panel_beta, "grp", 1)
    amps_joined = jnp.concatenate(amps_list, axis=1)
    panels_joined = jnp.concatenate(panel_list, axis=0)
    partial_value = jnp.dot(amps_joined, panels_joined, preferred_element_type=jnp.float32)
    summed = lax.psum_scatter(partial_value, "slab", scatter_dimension=0, tiled=True)
    grad_alpha = jnp.transpose(summed.reshape(virt_width, occ_count, aux_width), (1, 0, 2))
    grad_beta = lax.psum_scatter(beta_accum, "grp", scatter_dimension=0, tiled=True)
    return (grad_alpha, grad_beta)


def solution(mesh):
    in_specs = (P("grp", "slab", None), P("grp", "slab", None), P(), P(), P(), P())
    out_specs = (P("grp", "slab", None), P("grp", "slab", None))
    return jax.shard_map(body, mesh=mesh, in_specs=in_specs, out_specs=out_specs, check_vma=False)
```

profile of v0, /device:TPU:1, one launch (start us, length us, event | category | flops | bytes accessed | tf_op | source)
XLA Modules:
  0.0 507.4 jit_solution(9708389919537313207)
XLA Ops:
  10.1 15.0 %collective-permute-done = bf16[1,48,2560]{2,1,0:T(8,128)(2,1)S(1)} collective-permute-done((bf16[1,48,2560]{2,1,0:T(8,128)(2,1)}, bf16[1,48,2560]{2,1,0:T(8,128)(2,1)S(1)}, u32[]{:S(2)}, u32[]{:S(2)}) %collective-permute-start) | collective-permute-done | bytes 245792 | tf_op jit(solution)/shard_map/ppermute | solution.py:9
  25.1 19.2 %collective-permute-done.1 = bf16[1,48,2560]{2,1,0:T(8,128)(2,1)S(1)} collective-permute-done((bf16[1,48,2560]{2,1,0:T(8,128)(2,1)S(1)}, bf16[1,48,2560]{2,1,0:T(8,128)(2,1)S(1)}, u32[]{:S(2)}, u32[]{:S(2)}) %collective-permute-start.1) | collective-permute-done | bytes 245792 | tf_op jit(solution)/shard_map/ppermute | solution.py:9
  44.4 19.8 %collective-permute-done.2 = bf16[1,48,2560]{2,1,0:T(8,128)(2,1)S(1)} collective-permute-done((bf16[1,48,2560]{2,1,0:T(8,128)(2,1)S(1)}, bf16[1,48,2560]{2,1,0:T(8,128)(2,1)S(1)}, u32[]{:S(2)}, u32[]{:S(2)}) %collective-permute-start.2) | collective-permute-done | bytes 245792 | tf_op jit(solution)/shard_map/ppermute | solution.py:9
  64.2 20.8 %collective-permute-done.3 = bf16[1,48,2560]{2,1,0:T(8,128)(2,1)S(1)} collective-permute-done((bf16[1,48,2560]{2,1,0:T(8,128)(2,1)S(1)}, bf16[1,48,2560]{2,1,0:T(8,128)(2,1)S(1)}, u32[]{:S(2)}, u32[]{:S(2)}) %collective-permute-start.3) | collective-permute-done | bytes 245792 | tf_op jit(solution)/shard_map/ppermute | solution.py:9
  85.0 18.0 %collective-permute-done.4 = bf16[1,48,2560]{2,1,0:T(8,128)(2,1)S(1)} collective-permute-done((bf16[1,48,2560]{2,1,0:T(8,128)(2,1)S(1)}, bf16[1,48,2560]{2,1,0:T(8,128)(2,1)S(1)}, u32[]{:S(2)}, u32[]{:S(2)}) %collective-permute-start.4) | collective-permute-done | bytes 245792 | tf_op jit(solution)/shard_map/ppermute | solution.py:9
  106.6 12.3 %collective-permute-done.5 = bf16[1,48,2560]{2,1,0:T(8,128)(2,1)S(1)} collective-permute-done((bf16[1,48,2560]{2,1,0:T(8,128)(2,1)S(1)}, bf16[1,48,2560]{2,1,0:T(8,128)(2,1)S(1)}, u32[]{:S(2)}, u32[]{:S(2)}) %collective-permute-start.5) | collective-permute-done | bytes 245792 | tf_op jit(solution)/shard_map/ppermute | solution.py:9
  118.9 7.3 %constant_dynamic-update-slice_fusion.7 = (bf16[1536,384]{0,1:T(8,128)(2,1)S(1)}, bf16[1536,48]{0,1:T(8,128)(2,1)S(1)}) fusion(f32[]{:T(128)} %bitcast.5, f32[]{:T(128)} %bitcast.4, f32[48]{0:T(128)S(1)} %dynamic_slice.30, f32[1536]{0:T(1024)} %param.10, bf16[1,1536,2560]{2,1,0:T(8,128)(2,1)} %all-gather.2.cloned.1.call-done, bf16[1,48,2560]{2,1,0:T(8,128)(2,1)} %param.7), kind=kOutput, calls=%fused_computation.112 | convolution fusion | flops 377929728 | bytes 8411336 | tf_op jit(solution)/shard_map/iaq,jbq->aijb/dot_general | solution.py:22
  126.2 2.4 broadcast_in_dim.2
  130.8 3.5 constant_dynamic-update-slice_fusion.6
  134.3 2.3 fusion.41
  136.6 3.6 constant_dynamic-update-slice_fusion.5
  140.2 2.3 fusion.47
  142.4 3.6 constant_dynamic-update-slice_fusion.4
  148.3 3.6 constant_dynamic-update-slice_fusion.3
  151.9 2.3 fusion.59
  154.2 3.6 constant_dynamic-update-slice_fusion.2
  157.8 2.3 fusion.65
  160.0 3.5 constant_dynamic-update-slice_fusion.1
  163.6 2.5 fusion.71
  166.0 3.6 constant_dynamic-update-slice_fusion
  169.6 2.3 fusion.77
  173.0 7.9 %fusion.209 = f32[1536,2560]{1,0:T(8,128)} fusion(bf16[1536,384]{0,1:T(8,128)(2,1)S(1)} %get-tuple-element.24, bf16[384,2560]{1,0:T(8,128)(2,1)S(1)} %bitcast_dynamic-update-slice_fusion), kind=kOutput, calls=%fused_computation.114 | convolution fusion | flops 3019898880 | bytes 18874368 | tf_op jit(solution)/shard_map/dot_general | solution.py:55
  180.9 136.6 %reduce-scatter.5.cloned.1.call-done = f32[1,48,2560]{2,1,0:T(8,128)} async-done(((f32[8,48,2560]{2,1,0:T(8,128)}), f32[1,48,2560]{2,1,0:T(8,128)}) %reduce-scatter.5.cloned.1.call-update) | async-done | bytes 491536 | tf_op jit(solution)/shard_map/reduce_scatter | solution.py:58
  317.6 183.3 %reduce-scatter.3.cloned.1.call-done = f32[48,2560]{1,0:T(8,128)} async-done(((f32[1536,2560]{1,0:T(8,128)}), f32[48,2560]{1,0:T(8,128)}) %reduce-scatter.3.cloned.1.call-update) | async-done | bytes 491536 | tf_op jit(solution)/shard_map/reduce_scatter | solution.py:56
  (34 shorter events, 12.1 us)
Async XLA Ops:
  7.2 111.7 %all-gather.2.cloned.1.call-start = ((), (), s32[]{:S(2)}) async-start(), calls=%async_computation.2 | async-start | bytes 8110080 | tf_op jit(solution)/shard_map/all_gather | solution.py:21
  7.9 309.7 %reduce-scatter.5.cloned.1.call-start = ((), (), s32[]{:S(2)}) async-start(), calls=%async_computation.4 | async-start | bytes 4423680 | tf_op jit(solution)/shard_map/reduce_scatter | solution.py:58
  7.9 17.2 %collective-permute-start = (bf16[1,48,2560]{2,1,0:T(8,128)(2,1)}, bf16[1,48,2560]{2,1,0:T(8,128)(2,1)S(1)}, u32[]{:S(2)}, u32[]{:S(2)}) collective-permute-start(bf16[1,48,2560]{2,1,0:T(8,128)(2,1)} %param.7), channel_id=1, source_target_pairs={{0,32},{32,64},{64,96},{96,128},{128,160},{160,192},{192,224},{224... | collective-permute-start | bytes 737288 | tf_op jit(solution)/shard_map/ppermute | solution.py:9
  25.1 19.2 %collective-permute-start.1 = (bf16[1,48,2560]{2,1,0:T(8,128)(2,1)S(1)}, bf16[1,48,2560]{2,1,0:T(8,128)(2,1)S(1)}, u32[]{:S(2)}, u32[]{:S(2)}) collective-permute-start(bf16[1,48,2560]{2,1,0:T(8,128)(2,1)S(1)} %collective-permute-done), channel_id=1, source_target_pairs={{0,32},{32,64},{64,96},{96,128},{128,160},{160,192},{192,224},{224... | collective-permute-start | bytes 737288 | tf_op jit(solution)/shard_map/ppermute | solution.py:9
  44.4 19.8 %collective-permute-start.2 = (bf16[1,48,2560]{2,1,0:T(8,128)(2,1)S(1)}, bf16[1,48,2560]{2,1,0:T(8,128)(2,1)S(1)}, u32[]{:S(2)}, u32[]{:S(2)}) collective-permute-start(bf16[1,48,2560]{2,1,0:T(8,128)(2,1)S(1)} %collective-permute-done.1), channel_id=1, source_target_pairs={{0,32},{32,64},{64,96},{96,128},{128,160},{160,192},{192,224},{224... | collective-permute-start | bytes 737288 | tf_op jit(solution)/shard_map/ppermute | solution.py:9
  64.2 20.8 %collective-permute-start.3 = (bf16[1,48,2560]{2,1,0:T(8,128)(2,1)S(1)}, bf16[1,48,2560]{2,1,0:T(8,128)(2,1)S(1)}, u32[]{:S(2)}, u32[]{:S(2)}) collective-permute-start(bf16[1,48,2560]{2,1,0:T(8,128)(2,1)S(1)} %collective-permute-done.2), channel_id=1, source_target_pairs={{0,32},{32,64},{64,96},{96,128},{128,160},{160,192},{192,224},{224... | collective-permute-start | bytes 737288 | tf_op jit(solution)/shard_map/ppermute | solution.py:9
  85.0 18.0 %collective-permute-start.4 = (bf16[1,48,2560]{2,1,0:T(8,128)(2,1)S(1)}, bf16[1,48,2560]{2,1,0:T(8,128)(2,1)S(1)}, u32[]{:S(2)}, u32[]{:S(2)}) collective-permute-start(bf16[1,48,2560]{2,1,0:T(8,128)(2,1)S(1)} %collective-permute-done.3), channel_id=1, source_target_pairs={{0,32},{32,64},{64,96},{96,128},{128,160},{160,192},{192,224},{224... | collective-permute-start | bytes 737288 | tf_op jit(solution)/shard_map/ppermute | solution.py:9
  103.0 15.9 %collective-permute-start.5 = (bf16[1,48,2560]{2,1,0:T(8,128)(2,1)S(1)}, bf16[1,48,2560]{2,1,0:T(8,128)(2,1)S(1)}, u32[]{:S(2)}, u32[]{:S(2)}) collective-permute-start(bf16[1,48,2560]{2,1,0:T(8,128)(2,1)S(1)} %collective-permute-done.4), channel_id=1, source_target_pairs={{0,32},{32,64},{64,96},{96,128},{128,160},{160,192},{192,224},{224... | collective-permute-start | bytes 737288 | tf_op jit(solution)/shard_map/ppermute | solution.py:9
  118.9 47.1 %collective-permute-start.6 = (bf16[1,48,2560]{2,1,0:T(8,128)(2,1)S(1)}, bf16[1,48,2560]{2,1,0:T(8,128)(2,1)S(1)}, u32[]{:S(2)}, u32[]{:S(2)}) collective-permute-start(bf16[1,48,2560]{2,1,0:T(8,128)(2,1)S(1)} %collective-permute-done.5), channel_id=1, source_target_pairs={{0,32},{32,64},{64,96},{96,128},{128,160},{160,192},{192,224},{224... | collective-permute-start | bytes 737288 | tf_op jit(solution)/shard_map/ppermute | solution.py:9
  118.9 9.7 %copy-start = (bf16[1,1536,2560]{2,1,0:T(8,128)(2,1)S(1)}, bf16[1,1536,2560]{2,1,0:T(8,128)(2,1)}, u32[]{:S(2)}) copy-start(bf16[1,1536,2560]{2,1,0:T(8,128)(2,1)} %all-gather.2.cloned.1.call-done) | copy-start | bytes 23592964
  128.6 2.2 copy-start.2
  171.9 0.9 copy-start.1
  171.9 329.0 %reduce-scatter.3.cloned.1.call-start = ((), (), s32[]{:S(2)}) async-start(), calls=%async_computation.3 | async-start | bytes 16220160 | tf_op jit(solution)/shard_map/reduce_scatter | solution.py:56
Sparse Core Ops, SparseCore 0:
  9.8 72.5 all-gather.1
  172.0 145.4 reduce-scatter.4
  320.7 180.1 reduce-scatter.2
where the time goes:
time: 510 us; the launch traced here: 507 us
  waiting for transfers between devices  426 us (84%)
  matrix products  58.4 us (11%)
  between operations  13.9 us (3%)
  local copies, waits for them, and re-layouts  6.99 us (1%)
    reduce_scatter x1, waiting for transfers between devices, body(): lax.psum_scatter(partial_value, 'slab', scatter_dimension=0, tiled=True)  183 us
    reduce_scatter x1, waiting for transfers between devices, body(): lax.psum_scatter(beta_accum, 'grp', scatter_dimension=0, tiled=True)  137 us
    ppermute x7, waiting for transfers between devices, passed_along(): lax.ppermute(value, axis, [(i, (i + by) % length) for i in range(length)])  105 us
    dot_general x7, matrix products, body(): jnp.einsum('iaq,jbq->aijb', piece, panel_beta, preferred_element_type=jnp...  25 us
    dot_general x8, matrix products, body(): jnp.einsum('aijb,iaq->jbq', amplitudes, piece, preferred_element_type=jnp...  18.2 us
  transfers between devices with their start and end apart: 10, of which 8 were waited for; matrix products, arithmetic and copies ran while one was open for 12% of the time, Pallas kernels for 0%

commit v1 on v0

v1 whole, which is shorter than its diff:
```python
import functools

import jax
import jax.numpy as jnp
from jax import lax
from jax.experimental import pallas as pl
from jax.experimental.pallas import tpu as pltpu
from jax.sharding import PartitionSpec as P

MESH = pl.DeviceIdType.MESH
ROWS = 48
HALF = 1280
QUART = 640
BROWS = 768
POS = {0: 0, 1: 1, 7: 2, 2: 3, 6: 4, 3: 5, 5: 6, 4: 7}
SCALE = 512.0
TINY = 1e-37
F32 = jnp.float32
BF16 = jnp.bfloat16


def encode(value):
    scaled = value * SCALE
    square = scaled * jnp.abs(scaled)
    return (square * jnp.abs(square)).astype(BF16)


def decode(code):
    wide = code.astype(F32)
    size = jnp.abs(wide)
    root = lax.rsqrt(lax.rsqrt(jnp.maximum(size, TINY))) * (1.0 / SCALE)
    root = jnp.where(size > TINY, root, 0.0)
    return jnp.where(wide < 0.0, -root, root)


def kernel(
    occ_a, occ_b, virt_a, virt_b, a_hbm, b_hbm, ga_out, gb_out,
    A, B, I, T, TT, G, GBO, GBS, GBR, S1, R1A, R1B, S2, R2A, R2B, SZ, RZ, RZ0, VA,
    local_sem, send_sem, recv_sem,
):
    grp = lax.axis_index("grp")
    slab = lax.axis_index("slab")
    z_hi, y = grp // 4, grp % 4
    x, z_lo, core = slab // 8, (slab // 2) % 4, slab % 2
    z = z_hi * 4 + z_lo

    def device(dx=0, dy=0, dz=0, dc=0):
        nx, ny, nz, nc = (x + dx) % 4, (y + dy) % 4, (z + dz) % 8, (core + dc) % 2
        return ((nz // 4) * 4 + ny, nx * 8 + (nz % 4) * 2 + nc)

    xy = {(0, 1): device(dx=1), (0, -1): device(dx=3), (1, 1): device(dy=1), (1, -1): device(dy=3)}
    zdev = {1: device(dz=1), -1: device(dz=7)}
    sibling = device(dc=1)

    local = []
    for h in range(2):
        cols = pl.ds(h * HALF, HALF)
        local.append(pltpu.make_async_copy(a_hbm.at[0, :, cols], A.at[h, 0, 0], local_sem.at[h]))
        local.append(pltpu.make_async_copy(b_hbm.at[0, :, cols], B.at[h, pl.ds(0, ROWS)], local_sem.at[2 + h]))
    for copy in local:
        copy.start()

    barrier = pltpu.get_barrier_semaphore()
    for neighbour in list(xy.values()) + list(zdev.values()) + [sibling]:
        pl.semaphore_signal(barrier, inc=1, device_id=neighbour, device_id_type=MESH)

    eye = lax.broadcasted_iota(jnp.int32, (ROWS, ROWS), 0) == lax.broadcasted_iota(jnp.int32, (ROWS, ROWS), 1)
    for dx in range(4):
        row = virt_a[pl.ds(((x + dx) % 4) * 8 + z_lo * 2 + core, 1), :]
        column = jnp.sum(jnp.where(eye, jnp.broadcast_to(row, (ROWS, ROWS)), 0.0), axis=1, keepdims=True)
        VA[dx] = jnp.broadcast_to(column, (ROWS, 128))
    lanes = lax.broadcasted_iota(jnp.int32, (8, BROWS), 1)
    part = virt_b[pl.ds(x, 1), :]
    ring_virt = jnp.broadcast_to(jnp.concatenate([part, part], axis=1), (8, BROWS))
    ring_occ = jnp.where(lanes < 384, occ_b[y], occ_b[4 + y])
    vb = jnp.zeros((8, BROWS), F32)
    ob = jnp.zeros((8, BROWS), F32)
    for r, p in POS.items():
        there = (z + r) % 8
        for k in range(2):
            shift = (96 * p + 768 - 96 * there + (48 * core if k else 768 - 48 * core)) % 768
            here = (lanes >= 96 * p + 48 * k) & (lanes < 96 * p + 48 * k + 48)
            vb = jnp.where(here, pltpu.roll(ring_virt, shift, 1), vb)
            ob = jnp.where(here, pltpu.roll(ring_occ, shift, 1), ob)
    vb, ob = vb[0:1], ob[0:1]

    copies = {}

    def remote(name, src, dst, dev):
        index = len(copies)
        copies[name] = pltpu.make_async_remote_copy(
            src_ref=src, dst_ref=dst, send_sem=send_sem.at[index], recv_sem=recv_sem.at[index],
            device_id=dev, device_id_type=MESH,
        )

    def start(*names):
        for name in names:
            copies[name].start()

    def arrived(*names):
        for name in names:
            copies[name].wait_recv()

    def ablock(h, d1, d2):
        return A.at[0, d2, d1] if h == 0 else A.at[1, d1, d2]

    def bblock(h, r, k=0):
        return B.at[h, pl.ds(POS[r % 8] * 96 + k * ROWS, ROWS)]

    first, second = pl.ds(0, QUART), pl.ds(QUART, QUART)
    for h in range(2):
        one, two = h, 1 - h
        remote(("p1+", h), ablock(h, 0, 0), ablock(h, 3, 0), xy[one, 1])
        remote(("p1-", h), ablock(h, 0, 0), ablock(h, 1, 0), xy[one, -1])
        remote(("p1f+", h), ablock(h, 3, 0).at[:, first], ablock(h, 2, 0).at[:, first], xy[one, 1])
        remote(("p1f-", h), ablock(h, 1, 0).at[:, second], ablock(h, 2, 0).at[:, second], xy[one, -1])
        for u in range(4):
            remote(("p2+", h, u), ablock(h, u, 0), ablock(h, u, 3), xy[two, 1])
            remote(("p2-", h, u), ablock(h, u, 0), ablock(h, u, 1), xy[two, -1])
            if u % 2 == 0:
                remote(("p2f", h, u), ablock(h, u, 3), ablock(h, u, 2), xy[two, 1])
            else:
                remote(("p2f", h, u), ablock(h, u, 1), ablock(h, u, 2), xy[two, -1])
        for k in range(1, 4):
            remote(("z+", h, k), bblock(h, 1 - k), bblock(h, -k), zdev[1])
            remote(("z-", h, k), bblock(h, k - 1), bblock(h, k), zdev[-1])
        if h == 0:
            remote(("z4", h), bblock(h, 5), bblock(h, 4), zdev[1])
        else:
            remote(("z4", h), bblock(h, 3), bblock(h, 4), zdev[-1])
        for r in range(8):
            remote(("sib", h, r), bblock(h, r, 0), bblock(h, r, 1), sibling)

        for u in range(4):
            remote(("1a", h, u), S1.at[h, 2, u], R1A.at[h, u], xy[two, 1 if u % 2 == 0 else -1])
            remote(("1b+", h, u), S1.at[h, 1, u], R1B.at[h, 0, u], xy[two, 1])
            remote(("1b-", h, u), S1.at[h, 3, u], R1B.at[h, 1, u], xy[two, -1])
        remote(("2a+", h), S2.at[h, 2, :, first], R2A.at[h, :, first], xy[one, 1])
        remote(("2a-", h), S2.at[h, 2, :, second], R2A.at[h, :, second], xy[one, -1])
        remote(("2b+", h), S2.at[h, 1], R2B.at[h, 0], xy[one, 1])
        remote(("2b-", h), S2.at[h, 3], R2B.at[h, 1], xy[one, -1])
        if h == 0:
            remote(("rz", h, 4), SZ.at[h, 4], RZ.at[h, 3], zdev[1])
        else:
            remote(("rz", h, 4), SZ.at[h, 4], RZ.at[h, 5], zdev[-1])
        for r in (3, 2):
            remote(("rz", h, r), SZ.at[h, r], RZ.at[h, r - 1], zdev[1])
            remote(("rz", h, 8 - r), SZ.at[h, 8 - r], RZ.at[h, 9 - r], zdev[-1])
        remote(("rz", h, 1), SZ.at[h, 1], RZ0.at[h, 0], zdev[1])
        remote(("rz", h, 7), SZ.at[h, 7], RZ0.at[h, 1], zdev[-1])
        for p in range(8):
            remote(("gsib", h, p), GBS.at[h, p], GBR.at[h, p], sibling)

    def integrals(h, d2, j):
        left = (A[0, d2] if h == 0 else A[1, :, d2]).reshape(4 * ROWS, HALF)
        right = B[h, pl.ds(j * 256, 256), :]
        value = lax.dot_general(left, right, (((1,), (1,)), ((), ())), preferred_element_type=F32)
        value = value.reshape(4, ROWS, 256)
        if h == 0:
            I[0, d2, :, :, pl.ds(j * 256, 256)] = value
        else:
            I[1, :, d2, :, pl.ds(j * 256, 256)] = value

    def amplitudes(low, high):
        def one(block, carry):
            dy, dx = block // 4, block % 4
            occ = occ_a[z_hi * 4 + (y + dy) % 4]
            for tile in range(low, high):
                at = pl.ds(tile * 128, 128)
                number = I[0, dy, dx, :, at] + I[1, dy, dx, :, at]
                below = VA[dx] + vb[:, tile * 128:tile * 128 + 128] - occ - ob[:, tile * 128:tile * 128 + 128]
                T[dy, dx, :, at] = (-number / below).astype(BF16)
            return carry

        lax.fori_loop(0, 16, one, 0)
        for tile in range(low, high):
            square = T[:, :, :, pl.ds(tile * 128, 128)].reshape(BROWS, 128)
            TT[pl.ds(tile * 128, 128), :] = jnp.transpose(square.astype(F32)).astype(BF16)

    def alpha_term(h, d2):
        raw = {2: (0, 1, 2, 3), 1: (1, 3), 3: (0, 2), 0: ()}[d2]

        def one(j, carry):
            at = pl.ds(pl.multiple_of(j * 256, 256), 256)
            left = (T[d2] if h == 0 else T[:, d2]).reshape(4 * ROWS, BROWS)
            value = jnp.dot(left, B[h, :, at], preferred_element_type=F32)
            for u in range(4):
                block = value[u * ROWS:(u + 1) * ROWS]
                if u in raw:
                    S1[h, d2, u, :, at] = encode(block)
                else:
                    G[h, d2, u, :, at] = block
            return carry

        lax.fori_loop(0, 5, one, 0)

    def beta_term(h, low, high):
        def one(j, carry):
            at = pl.ds(pl.multiple_of(j * 256, 256), 256)
            right = A[h, :, :, :, at].reshape(BROWS, 256)
            value = jnp.dot(TT[pl.ds(low * 96, (high - low) * 96), :], right, preferred_element_type=F32)
            for p in range(low, high):
                base = (p - low) * 96
                GBO[h, p, :, at] = value[base:base + ROWS]
                GBS[h, p, :, at] = value[base + ROWS:base + 2 * ROWS]
            return carry

        lax.fori_loop(0, 5, one, 0)
        for p in range(low, high):
            start(("gsib", h, p))

    def by_rows(body):
        def one(step, carry):
            body(pl.ds(pl.multiple_of(step * 16, 16), 16))
            return carry

        lax.fori_loop(0, ROWS // 16, one, 0)

    for copy in local:
        copy.wait()
    pl.semaphore_wait(barrier, 7)
    H = (0, 1)
    for h in H:
        start(("p1+", h), ("p1-", h))
    for h in H:
        start(("z+", h, 1), ("z-", h, 1))
    for h in H:
        start(("p2+", h, 0), ("p2-", h, 0))
    for h in H:
        start(("sib", h, 0))
    for h in H:
        arrived(("p1+", h), ("p1-", h))
        start(("p1f+", h), ("p1f-", h))
    for u in (3, 1):
        for h in H:
            start(("p2+", h, u), ("p2-", h, u))
    for h in H:
        arrived(("z+", h, 1), ("z-", h, 1))
        start(("z+", h, 2), ("z-", h, 2), ("sib", h, 1), ("sib", h, 7))
    for h in H:
        arrived(("p1f+", h), ("p1f-", h))
        start(("p2+", h, 2), ("p2-", h, 2))
    for h in H:
        arrived(("p2+", h, 0), ("p2-", h, 0))
        start(("p2f", h, 0))
    for h in H:
        arrived(("sib", h, 0), ("sib", h, 1), ("sib", h, 7))
        integrals(h, 0, 0)
    for h in H:
        arrived(("z+", h, 2), ("z-", h, 2))
        start(("z+", h, 3), ("z-", h, 3), ("sib", h, 2), ("sib", h, 6))
    for u in (3, 1):
        for h in H:
            arrived(("p2+", h, u), ("p2-", h, u))
            start(("p2f", h, u))
    for h in H:
        arrived(("p2+", h, 2), ("p2-", h, 2))
        start(("p2f", h, 2))
    for h in H:
        integrals(h, 1, 0)
        integrals(h, 3, 0)
    for h in H:
        arrived(("z+", h, 3), ("z-", h, 3))
        start(("z4", h), ("sib", h, 3), ("sib", h, 5))
    for h in H:
        arrived(("sib", h, 2), ("sib", h, 6), ("sib", h, 3))
        for d2 in (0, 1, 3):
            integrals(h, d2, 1)
    for h in H:
        for u in (0, 3, 1, 2):
            arrived(("p2f", h, u))
        integrals(h, 2, 0)
        integrals(h, 2, 1)
    for h in H:
        arrived(("z4", h))
        start(("sib", h, 4))
    amplitudes(0, 4)
    for h in H:
        arrived(("sib", h, 5), ("sib", h, 4))
        for d2 in range(4):
            integrals(h, d2, 2)
    amplitudes(4, 6)

    def add_first(h, u):
        d2 = 1 if u % 2 == 0 else 3
        arrived(("1a", h, u))

        def body(rows):
            S1[h, d2, u, rows] = encode(G[h, d2, u, rows] + decode(R1A[h, u, rows]))

        by_rows(body)
        start(("1b+" if d2 == 1 else "1b-", h, u))

    def plane_sum(h, u, rows):
        return G[h, 0, u, rows] + decode(R1B[h, 0, u, rows]) + decode(R1B[h, 1, u, rows])

    def z_send(h, r):
        p = POS[r]
        chained = r in (1, 2, 6, 7) or (r, h) in ((3, 0), (5, 1))
        arrived(("gsib", h, p))
        if r == 3 and h == 0 or r == 5 and h == 1:
            arrived(("rz", h, 4))
        elif chained:
            arrived(("rz", h, r + 1 if r < 4 else r - 1))

        def body(rows):
            value = GBO[h, p, rows] + GBR[h, p, rows]
            if chained:
                value = value + decode(RZ[h, r, rows])
            SZ[h, r, rows] = encode(value)

        by_rows(body)
        start(("rz", h, r))

    order = (2, 1, 3, 0)
    for h in H:
        alpha_term(h, 2)
        for u in order:
            start(("1a", h, u))
    for h in H:
        beta_term(h, 7, 8)
    for h in H:
        alpha_term(h, 1)
        start(("1b+", h, 1), ("1b+", h, 3))
    for h in H:
        z_send(h, 4)
    for h in H:
        alpha_term(h, 3)
        start(("1b-", h, 2), ("1b-", h, 0))
    for h in H:
        beta_term(h, 5, 7)
    z_send(1, 3)
    z_send(0, 5)
    for h in H:
        add_first(h, 2)
    z_send(0, 3)
    z_send(1, 5)
    for u in (1, 3, 0):
        for h in H:
            add_first(h, u)
    for h in H:
        beta_term(h, 3, 5)
    for h in H:
        alpha_term(h, 0)
    for h in H:
        z_send(h, 2)
        z_send(h, 6)
    for h in H:
        beta_term(h, 1, 3)
    for h in H:
        beta_term(h, 0, 1)

    for h in H:
        arrived(("1b+", h, 2), ("1b-", h, 2))

        def body(rows):
            S2[h, 2, rows] = encode(plane_sum(h, 2, rows))

        by_rows(body)
        start(("2a+", h), ("2a-", h))
    for h in H:
        z_send(h, 1)
        z_send(h, 7)
    for h in H:
        for u in (1, 3):
            arrived(("1b+", h, u), ("1b-", h, u))

            def body(rows):
                G[h, 0, u, rows] = plane_sum(h, u, rows)

            by_rows(body)
    for h in H:
        for u in (1, 3):
            arrived(("2a+" if u == 1 else "2a-", h))
            added, plain = (first, second) if u == 1 else (second, first)

            def body(rows):
                S2[h, u, rows, added] = encode(G[h, 0, u, rows, added] + decode(R2A[h, rows, added]))
                S2[h, u, rows, plain] = encode(G[h, 0, u, rows, plain])

            by_rows(body)
            start(("2b+" if u == 1 else "2b-", h))
    for h in H:
        arrived(("1b+", h, 0), ("1b-", h, 0))

        def body(rows):
            G[h, 0, 0, rows] = plane_sum(h, 0, rows)

        by_rows(body)
    for h in H:
        arrived(("gsib", h, 0), ("rz", h, 1), ("rz", h, 7))

        def body(rows):
            gb_out[0, rows, pl.ds(h * HALF, HALF)] = (
                GBO[h, 0, rows] + GBR[h, 0, rows] + decode(RZ0[h, 0, rows]) + decode(RZ0[h, 1, rows])
            )

        by_rows(body)
    for h in H:
        arrived(("2b+", h), ("2b-", h))

        def body(rows):
            ga_out[0, rows, pl.ds(h * HALF, HALF)] = (
                G[h, 0, 0, rows] + decode(R2B[h, 0, rows]) + decode(R2B[h, 1, rows])
            )

        by_rows(body)
    for copy in copies.values():
        copy.wait_send()


def body(orbital_alpha, orbital_beta, occ_alpha, occ_beta, virt_alpha, virt_beta):
    block = (ROWS, HALF)
    smem = pl.BlockSpec(memory_space=pltpu.SMEM)
    vmem = pl.BlockSpec(memory_space=pltpu.VMEM)
    hbm = pl.BlockSpec(memory_space=pl.ANY)
    out = jax.ShapeDtypeStruct((1, ROWS, 2 * HALF), F32)
    count = 128
    return pl.pallas_call(
        kernel,
        out_shape=(out, out),
        in_specs=[smem, smem, vmem, vmem, hbm, hbm],
        out_specs=(vmem, vmem),
        scratch_shapes=[
            pltpu.VMEM((2, 4, 4) + block, BF16),
            pltpu.VMEM((2, BROWS, HALF), BF16),
            pltpu.VMEM((2, 4, 4, ROWS, BROWS), F32),
            pltpu.VMEM((4, 4, ROWS, BROWS), BF16),
            pltpu.VMEM((BROWS, BROWS), BF16),
            pltpu.VMEM((2, 4, 4) + block, F32),
            pltpu.VMEM((2, 8) + block, F32),
            pltpu.VMEM((2, 8) + block, F32),
            pltpu.VMEM((2, 8) + block, F32),
            pltpu.VMEM((2, 4, 4) + block, BF16),
            pltpu.VMEM((2, 4) + block, BF16),
            pltpu.VMEM((2, 2, 4) + block, BF16),
            pltpu.VMEM((2, 4) + block, BF16),
            pltpu.VMEM((2,) + block, BF16),
            pltpu.VMEM((2, 2) + block, BF16),
            pltpu.VMEM((2, 8) + block, BF16),
            pltpu.VMEM((2, 8) + block, BF16),
            pltpu.VMEM((2, 2) + block, BF16),
            pltpu.VMEM((4, ROWS, 128), F32),
            pltpu.SemaphoreType.DMA((4,)),
            pltpu.SemaphoreType.DMA((count,)),
            pltpu.SemaphoreType.DMA((count,)),
        ],
        compiler_params=pltpu.CompilerParams(
            collective_id=0, has_side_effects=True, vmem_limit_bytes=66 * 1000 * 1000
        ),
    )(occ_alpha, occ_beta, virt_alpha.reshape(32, ROWS), virt_beta.reshape(4, 384), orbital_alpha, orbital_beta)


def solution(mesh):
    in_specs = (P("grp", "slab", None), P("grp", "slab", None), P(), P(), P(), P())
    out_specs = (P("grp", "slab", None), P("grp", "slab", None))
    return jax.shard_map(body, mesh=mesh, in_specs=in_specs, out_specs=out_specs, check_vma=False)
```

time: 510 us -> 81.6 us (0.16)
  waiting for transfers between devices: 426 us -> 0 us
  Pallas kernels: 0 us -> 76.1 us
  matrix products: 58.4 us -> 0 us
  between operations: 13.9 us -> 0.66 us
    reduce_scatter x2 -> x0, waiting for transfers between devices: 320 us -> none  [the longest x1 183 us: body(): lax.psum_scatter(partial_value, 'slab', scatter_dimension=0, tiled=True)]
    ppermute x7 -> x0, waiting for transfers between devices: 105 us -> none  [passed_along(): lax.ppermute(value, axis, [(i, (i + by) % length) for i in range(length)])]
    pallas_call x0 -> x1, Pallas kernels: none -> 76.1 us  [body(): pl.pallas_call(kernel, out_shape=(out, out), in_specs=[smem, smem, vmem,...]
    dot_general x17 -> x0, matrix products: 58.4 us -> none  [the longest x7 25 us: body(): jnp.einsum('iaq,jbq->aijb', piece, panel_beta, preferred_element_type=jnp...]
  transfers between devices with their start and end apart: 10 -> 0, of which waited for: 8 -> 0; matrix products, arithmetic and copies ran while one was open for 12% -> 0% of each run, Pallas kernels for 0% -> 0%
where the time goes in v1:
time: 81.6 us; the launch traced here: 81.4 us
  Pallas kernels  76.1 us (93%)
  local copies, waits for them, and re-layouts  4.67 us (6%)
    pallas_call x1, Pallas kernels, body(): pl.pallas_call(kernel, out_shape=(out, out), in_specs=[smem, smem, vmem,...  76.1 us
    unnamed x6, local copies, waits for them, and re-layouts  2.68 us

profile of v1, /device:TPU:1, one launch (start us, length us, event | category | flops | bytes accessed | tf_op | source)
XLA Modules:
  0.0 81.4 jit_solution(6556706935764063466)
XLA Ops:
  0.6 0.0 copy-start.1
  0.6 1.3 %reshape.11.virt_b = f32[4,384]{1,0:T(4,128)} reshape(f32[1536]{0:T(1024)} %param.11) | data formatting | bytes 12288 | tf_op jit(solution)/shard_map/reshape | solution.py:451
  1.9 0.0 copy-done.1
  1.9 0.7 reshape.10.virt_a
  2.6 76.1 %shard_map.77 = (f32[1,48,2560]{2,1,0:T(8,128)}, f32[1,48,2560]{2,1,0:T(8,128)}) custom-call(f32[8]{0:T(128)} %occ_a.1, f32[8]{0:T(128)} %occ_b.1, f32[32,48]{1,0:T(8,128)} %reshape.10.virt_a, f32[4,384]{1,0:T(4,128)} %reshape.11.virt_b, bf16[1,48,2560]{2,1,0:T(8,128)(2,1)} %a_hbm.1, bf16[1,48,2560]{2,1,0:T(8,128)(2,1)} %b_hbm.1), custom_call_target="tpu_custom_call" | custom-call | tf_op jit(solution)/shard_map/pallas_call | solution.py:419
  78.7 0.0 copy-start
  78.7 1.9 %copy.10 = f32[1,48,2560]{2,1,0:T(8,128)} copy(f32[1,48,2560]{2,1,0:T(8,128)} %get-tuple-element.4) | data formatting | bytes 983040
  80.6 0.0 copy-done
  80.6 0.8 copy.11
Async XLA Ops:
  0.6 1.3 %copy-start.1 = (f32[1536]{0:T(1024)S(1)}, f32[1536]{0:T(1024)}, u32[]{:S(2)}) copy-start(f32[1536]{0:T(1024)} %param.10) | copy-start | bytes 18436
  78.7 1.9 %copy-start = (f32[1,48,2560]{2,1,0:T(8,128)S(1)}, f32[1,48,2560]{2,1,0:T(8,128)}, u32[]{:S(2)}) copy-start(f32[1,48,2560]{2,1,0:T(8,128)} %get-tuple-element.5) | copy-start | bytes 1474564

commit v2 on v1

--- a/solution.py
+++ b/solution.py
@@ -64,13 +64,18 @@
     for neighbour in list(xy.values()) + list(zdev.values()) + [sibling]:
         pl.semaphore_signal(barrier, inc=1, device_id=neighbour, device_id_type=MESH)
 
-    eye = lax.broadcasted_iota(jnp.int32, (ROWS, ROWS), 0) == lax.broadcasted_iota(jnp.int32, (ROWS, ROWS), 1)
+    eye = lax.broadcasted_iota(jnp.int32, (ROWS, 128), 0) == lax.broadcasted_iota(jnp.int32, (ROWS, 128), 1)
+
+    def energies(ref, column):
+        return jnp.concatenate([ref[pl.ds(3 * column + i, 1), :] for i in range(3)], axis=1)
+
     for dx in range(4):
-        row = virt_a[pl.ds(((x + dx) % 4) * 8 + z_lo * 2 + core, 1), :]
-        column = jnp.sum(jnp.where(eye, jnp.broadcast_to(row, (ROWS, ROWS)), 0.0), axis=1, keepdims=True)
+        row = jnp.broadcast_to(energies(virt_a, (x + dx) % 4), (8, 384))
+        row = pltpu.roll(row, (384 - 96 * z_lo - 48 * core) % 384, 1)[0:1, :128]
+        column = jnp.sum(jnp.where(eye, jnp.broadcast_to(row, (ROWS, 128)), 0.0), axis=1, keepdims=True)
         VA[dx] = jnp.broadcast_to(column, (ROWS, 128))
     lanes = lax.broadcasted_iota(jnp.int32, (8, BROWS), 1)
-    part = virt_b[pl.ds(x, 1), :]
+    part = energies(virt_b, x)
     ring_virt = jnp.broadcast_to(jnp.concatenate([part, part], axis=1), (8, BROWS))
     ring_occ = jnp.where(lanes < 384, occ_b[y], occ_b[4 + y])
     vb = jnp.zeros((8, BROWS), F32)
@@ -192,7 +197,7 @@
                     G[h, d2, u, :, at] = block
             return carry
 
-        lax.fori_loop(0, 5, one, 0)
+        lax.fori_loop(0, 5, one, 0, unroll=True)
 
     def beta_term(h, low, high):
         def one(j, carry):
@@ -205,7 +210,7 @@
                 GBS[h, p, :, at] = value[base + ROWS:base + 2 * ROWS]
             return carry
 
-        lax.fori_loop(0, 5, one, 0)
+        lax.fori_loop(0, 5, one, 0, unroll=True)
         for p in range(low, high):
             start(("gsib", h, p))
 
@@ -448,7 +453,7 @@
         compiler_params=pltpu.CompilerParams(
             collective_id=0, has_side_effects=True, vmem_limit_bytes=66 * 1000 * 1000
         ),
-    )(occ_alpha, occ_beta, virt_alpha.reshape(32, ROWS), virt_beta.reshape(4, 384), orbital_alpha, orbital_beta)
+    )(occ_alpha, occ_beta, virt_alpha.reshape(12, 128), virt_beta.reshape(12, 128), orbital_alpha, orbital_beta)
 
 
 def solution(mesh):

time: 81.6 us -> 72.6 us (0.89)
  Pallas kernels: 76.1 us -> 68.8 us
  local copies, waits for them, and re-layouts: 4.67 us -> 2.68 us
    pallas_call x1, Pallas kernels: 76.1 us -> 68.8 us  [body(): pl.pallas_call(kernel, out_shape=(out, out), in_specs=[smem, smem, vmem,...]
    reshape x2 -> x0, local copies, waits for them, and re-layouts: 1.98 us -> none  [the longest x1 1.3 us: body(): virt_beta.reshape(4, 384)]
    unnamed x6 -> x4, local copies, waits for them, and re-layouts: 2.68 us -> 2.68 us
where the time goes in v2:
time: 72.6 us; the launch traced here: 72.1 us
  Pallas kernels  68.8 us (95%)
  local copies, waits for them, and re-layouts  2.68 us (4%)
    pallas_call x1, Pallas kernels, body(): pl.pallas_call(kernel, out_shape=(out, out), in_specs=[smem, smem, vmem,...  68.8 us
    unnamed x4, local copies, waits for them, and re-layouts  2.68 us

profile of v2, /device:TPU:1, one launch (start us, length us, event | category | flops | bytes accessed | tf_op | source)
XLA Modules:
  0.0 72.1 jit_solution(17660547564779546817)
XLA Ops:
  0.6 68.8 %shard_map.77 = (f32[1,48,2560]{2,1,0:T(8,128)}, f32[1,48,2560]{2,1,0:T(8,128)}) custom-call(f32[8]{0:T(128)} %occ_a.1, f32[8]{0:T(128)} %occ_b.1, f32[12,128]{1,0:T(8,128)} %bitcast.2, f32[12,128]{1,0:T(8,128)} %bitcast.3, bf16[1,48,2560]{2,1,0:T(8,128)(2,1)} %a_hbm.1, bf16[1,48,2560]{2,1,0:T(8,128)(2,1)} %b_hbm.1), custom_call_target="tpu_custom_call" | custom-call | tf_op jit(solution)/shard_map/pallas_call | solution.py:424
  69.5 0.0 copy-start
  69.5 1.9 %copy.10 = f32[1,48,2560]{2,1,0:T(8,128)} copy(f32[1,48,2560]{2,1,0:T(8,128)} %get-tuple-element.4) | data formatting | bytes 983040
  71.4 0.0 copy-done
  71.4 0.8 %copy.11 = f32[1,48,2560]{2,1,0:T(8,128)} copy(f32[1,48,2560]{2,1,0:T(8,128)S(1)} %copy-done) | data formatting | bytes 983040
Async XLA Ops:
  69.5 1.9 %copy-start = (f32[1,48,2560]{2,1,0:T(8,128)S(1)}, f32[1,48,2560]{2,1,0:T(8,128)}, u32[]{:S(2)}) copy-start(f32[1,48,2560]{2,1,0:T(8,128)} %get-tuple-element.5) | copy-start | bytes 1474564

commit v3 on v2

--- a/solution.py
+++ b/solution.py
@@ -13,30 +13,16 @@
 QUART = 640
 BROWS = 768
 POS = {0: 0, 1: 1, 7: 2, 2: 3, 6: 4, 3: 5, 5: 6, 4: 7}
-SCALE = 512.0
+SCALE = 2.0**41
 TINY = 1e-37
 F32 = jnp.float32
 BF16 = jnp.bfloat16
 
 
-def encode(value):
-    scaled = value * SCALE
-    square = scaled * jnp.abs(scaled)
-    return (square * jnp.abs(square)).astype(BF16)
-
-
-def decode(code):
-    wide = code.astype(F32)
-    size = jnp.abs(wide)
-    root = lax.rsqrt(lax.rsqrt(jnp.maximum(size, TINY))) * (1.0 / SCALE)
-    root = jnp.where(size > TINY, root, 0.0)
-    return jnp.where(wide < 0.0, -root, root)
-
-
 def kernel(
     occ_a, occ_b, virt_a, virt_b, a_hbm, b_hbm, ga_out, gb_out,
     A, B, I, T, TT, G, GBO, GBS, GBR, S1, R1A, R1B, S2, R2A, R2B, SZ, RZ, RZ0, VA,
-    local_sem, send_sem, recv_sem,
+    OUT, out_sem, local_sem, send_sem, recv_sem,
 ):
     grp = lax.axis_index("grp")
     slab = lax.axis_index("slab")
@@ -156,31 +142,54 @@
         for p in range(8):
             remote(("gsib", h, p), GBS.at[h, p], GBR.at[h, p], sibling)
 
-    def integrals(h, d2, j):
+    def encode(value):
+        scaled = value * SCALE
+        return (scaled * jnp.abs(scaled)).astype(BF16)
+
+    def decode(code):
+        wide = code.astype(F32)
+        return wide * lax.rsqrt(jnp.maximum(jnp.abs(wide), TINY)) * (1.0 / SCALE)
+
+    def integrals(h, d2, low, width):
         left = (A[0, d2] if h == 0 else A[1, :, d2]).reshape(4 * ROWS, HALF)
-        right = B[h, pl.ds(j * 256, 256), :]
+        right = B[h, pl.ds(low, width), :]
         value = lax.dot_general(left, right, (((1,), (1,)), ((), ())), preferred_element_type=F32)
-        value = value.reshape(4, ROWS, 256)
+        value = value.reshape(4, ROWS, width)
         if h == 0:
-            I[0, d2, :, :, pl.ds(j * 256, 256)] = value
+            I[0, d2, :, :, pl.ds(low, width)] = value
         else:
-            I[1, :, d2, :, pl.ds(j * 256, 256)] = value
+            I[1, :, d2, :, pl.ds(low, width)] = value
+
+    def ratio(number, dy, dx, tile):
+        lanes = slice(tile * 128, tile * 128 + 128)
+        below = VA[dx] + vb[:, lanes] - occ_a[z_hi * 4 + (y + dy) % 4] - ob[:, lanes]
+        return (-number / below).astype(BF16)
+
+    def transpose(tile):
+        square = T[:, :, :, pl.ds(tile * 128, 128)].reshape(BROWS, 128)
+        TT[pl.ds(tile * 128, 128), :] = jnp.transpose(square.astype(F32)).astype(BF16)
 
     def amplitudes(low, high):
         def one(block, carry):
             dy, dx = block // 4, block % 4
-            occ = occ_a[z_hi * 4 + (y + dy) % 4]
             for tile in range(low, high):
                 at = pl.ds(tile * 128, 128)
-                number = I[0, dy, dx, :, at] + I[1, dy, dx, :, at]
-                below = VA[dx] + vb[:, tile * 128:tile * 128 + 128] - occ - ob[:, tile * 128:tile * 128 + 128]
-                T[dy, dx, :, at] = (-number / below).astype(BF16)
+                T[dy, dx, :, at] = ratio(I[0, dy, dx, :, at] + I[1, dy, dx, :, at], dy, dx, tile)
             return carry
 
         lax.fori_loop(0, 16, one, 0)
         for tile in range(low, high):
-            square = T[:, :, :, pl.ds(tile * 128, 128)].reshape(BROWS, 128)
-            TT[pl.ds(tile * 128, 128), :] = jnp.transpose(square.astype(F32)).astype(BF16)
+            transpose(tile)
+
+    def last_amplitudes(dy):
+        at = pl.ds(640, 128)
+        value = None
+        for h in range(2):
+            left = A[h, dy].reshape(4 * ROWS, HALF)
+            term = lax.dot_general(left, B[h, at, :], (((1,), (1,)), ((), ())), preferred_element_type=F32)
+            value = term if value is None else value + term
+        for dx in range(4):
+            T[dy, dx, :, at] = ratio(value[dx * ROWS:(dx + 1) * ROWS], dy, dx, 5)
 
     def alpha_term(h, d2):
         raw = {2: (0, 1, 2, 3), 1: (1, 3), 3: (0, 2), 0: ()}[d2]
@@ -250,7 +259,7 @@
         start(("p2f", h, 0))
     for h in H:
         arrived(("sib", h, 0), ("sib", h, 1), ("sib", h, 7))
-        integrals(h, 0, 0)
+        integrals(h, 0, 0, 256)
     for h in H:
         arrived(("z+", h, 2), ("z-", h, 2))
         start(("z+", h, 3), ("z-", h, 3), ("sib", h, 2), ("sib", h, 6))
@@ -262,29 +271,41 @@
         arrived(("p2+", h, 2), ("p2-", h, 2))
         start(("p2f", h, 2))
     for h in H:
-        integrals(h, 1, 0)
-        integrals(h, 3, 0)
+        integrals(h, 1, 0, 256)
+        integrals(h, 3, 0, 256)
     for h in H:
         arrived(("z+", h, 3), ("z-", h, 3))
         start(("z4", h), ("sib", h, 3), ("sib", h, 5))
     for h in H:
         arrived(("sib", h, 2), ("sib", h, 6), ("sib", h, 3))
         for d2 in (0, 1, 3):
-            integrals(h, d2, 1)
+            integrals(h, d2, 256, 256)
+    for h in H:
+        arrived(("sib", h, 5))
+        for d2 in (0, 1, 3):
+            integrals(h, d2, 512, 128)
+    for h in H:
+        arrived(("z4", h))
+        start(("sib", h, 4))
     for h in H:
         for u in (0, 3, 1, 2):
             arrived(("p2f", h, u))
-        integrals(h, 2, 0)
-        integrals(h, 2, 1)
-    for h in H:
-        arrived(("z4", h))
-        start(("sib", h, 4))
-    amplitudes(0, 4)
-    for h in H:
-        arrived(("sib", h, 5), ("sib", h, 4))
-        for d2 in range(4):
-            integrals(h, d2, 2)
-    amplitudes(4, 6)
+        integrals(h, 2, 0, 256)
+        integrals(h, 2, 256, 256)
+        integrals(h, 2, 512, 128)
+    amplitudes(0, 5)
+    for h in H:
+        arrived(("sib", h, 4))
+    for dy in (2, 1, 3, 0):
+        last_amplitudes(dy)
+    transpose(5)
+
+    outward = {}
+
+    def put(which, h):
+        target = (ga_out, gb_out)[which].at[0, :, pl.ds(h * HALF, HALF)]
+        outward[which, h] = pltpu.make_async_copy(OUT.at[which, h], target, out_sem.at[which, h])
+        outward[which, h].start()
 
     def add_first(h, u):
         d2 = 1 if u % 2 == 0 else 3
@@ -317,22 +338,44 @@
         by_rows(body)
         start(("rz", h, r))
 
-    order = (2, 1, 3, 0)
+    def second_far(h):
+        arrived(("1b+", h, 2), ("1b-", h, 2))
+
+        def body(rows):
+            S2[h, 2, rows] = encode(plane_sum(h, 2, rows))
+
+        by_rows(body)
+        start(("2a+", h), ("2a-", h))
+
+    def second_near(h, u):
+        arrived(("1b+", h, u), ("1b-", h, u))
+        arrived(("2a+" if u == 1 else "2a-", h))
+        added, plain = (first, second) if u == 1 else (second, first)
+
+        def body(rows):
+            value = plane_sum(h, u, rows)
+            S2[h, u, rows, plain] = encode(value[:, :QUART] if u == 3 else value[:, QUART:])
+            value = value[:, QUART:] if u == 3 else value[:, :QUART]
+            S2[h, u, rows, added] = encode(value + decode(R2A[h, rows, added]))
+
+        by_rows(body)
+        start(("2b+" if u == 1 else "2b-", h))
+
+    for h in H:
+        beta_term(h, 7, 8)
     for h in H:
         alpha_term(h, 2)
-        for u in order:
+        for u in (2, 1, 3, 0):
             start(("1a", h, u))
     for h in H:
-        beta_term(h, 7, 8)
+        z_send(h, 4)
     for h in H:
         alpha_term(h, 1)
         start(("1b+", h, 1), ("1b+", h, 3))
     for h in H:
-        z_send(h, 4)
-    for h in H:
         alpha_term(h, 3)
         start(("1b-", h, 2), ("1b-", h, 0))
-    for h in H:
+    for h in (1, 0):
         beta_term(h, 5, 7)
     z_send(1, 3)
     z_send(0, 5)
@@ -343,48 +386,27 @@
     for u in (1, 3, 0):
         for h in H:
             add_first(h, u)
-    for h in H:
+    for h in (1, 0):
         beta_term(h, 3, 5)
     for h in H:
         alpha_term(h, 0)
-    for h in H:
-        z_send(h, 2)
-        z_send(h, 6)
+    z_send(1, 2)
+    z_send(0, 6)
+    z_send(0, 2)
+    z_send(1, 6)
     for h in H:
         beta_term(h, 1, 3)
     for h in H:
         beta_term(h, 0, 1)
-
-    for h in H:
-        arrived(("1b+", h, 2), ("1b-", h, 2))
-
-        def body(rows):
-            S2[h, 2, rows] = encode(plane_sum(h, 2, rows))
-
-        by_rows(body)
-        start(("2a+", h), ("2a-", h))
-    for h in H:
-        z_send(h, 1)
-        z_send(h, 7)
-    for h in H:
-        for u in (1, 3):
-            arrived(("1b+", h, u), ("1b-", h, u))
-
-            def body(rows):
-                G[h, 0, u, rows] = plane_sum(h, u, rows)
-
-            by_rows(body)
-    for h in H:
-        for u in (1, 3):
-            arrived(("2a+" if u == 1 else "2a-", h))
-            added, plain = (first, second) if u == 1 else (second, first)
-
-            def body(rows):
-                S2[h, u, rows, added] = encode(G[h, 0, u, rows, added] + decode(R2A[h, rows, added]))
-                S2[h, u, rows, plain] = encode(G[h, 0, u, rows, plain])
-
-            by_rows(body)
-            start(("2b+" if u == 1 else "2b-", h))
+    for h in H:
+        second_far(h)
+    z_send(1, 1)
+    z_send(0, 7)
+    z_send(0, 1)
+    z_send(1, 7)
+    for h in H:
+        second_near(h, 1)
+        second_near(h, 3)
     for h in H:
         arrived(("1b+", h, 0), ("1b-", h, 0))
 
@@ -396,22 +418,46 @@
         arrived(("gsib", h, 0), ("rz", h, 1), ("rz", h, 7))
 
         def body(rows):
-            gb_out[0, rows, pl.ds(h * HALF, HALF)] = (
+            OUT[1, h, rows] = (
                 GBO[h, 0, rows] + GBR[h, 0, rows] + decode(RZ0[h, 0, rows]) + decode(RZ0[h, 1, rows])
             )
 
         by_rows(body)
+        put(1, h)
     for h in H:
         arrived(("2b+", h), ("2b-", h))
 
         def body(rows):
-            ga_out[0, rows, pl.ds(h * HALF, HALF)] = (
+            OUT[0, h, rows] = (
                 G[h, 0, 0, rows] + decode(R2B[h, 0, rows]) + decode(R2B[h, 1, rows])
             )
 
         by_rows(body)
+        put(0, h)
+    for copy in list(outward.values()):
+        copy.wait()
     for copy in copies.values():
         copy.wait_send()
+
+
+def hand_over(ga_in, gb_in, ga_out, gb_out, held, in_sem, out_sem):
+    pairs = [(w, h) for h in range(2) for w in range(2)]
+    source, target = (ga_in, gb_in), (ga_out, gb_out)
+    inward = [
+        pltpu.make_async_copy(source[w].at[0, :, pl.ds(h * HALF, HALF)], held.at[w, h], in_sem.at[w, h])
+        for w, h in pairs
+    ]
+    outward = [
+        pltpu.make_async_copy(held.at[w, h], target[w].at[0, :, pl.ds(h * HALF, HALF)], out_sem.at[w, h])
+        for w, h in pairs
+    ]
+    for copy in inward:
+        copy.start()
+    for before, after in zip(inward, outward):
+        before.wait()
+        after.start()
+    for copy in outward:
+        copy.wait()
 
 
 def body(orbital_alpha, orbital_beta, occ_alpha, occ_beta, virt_alpha, virt_beta):
@@ -421,11 +467,11 @@
     hbm = pl.BlockSpec(memory_space=pl.ANY)
     out = jax.ShapeDtypeStruct((1, ROWS, 2 * HALF), F32)
     count = 128
-    return pl.pallas_call(
+    sums = pl.pallas_call(
         kernel,
         out_shape=(out, out),
         in_specs=[smem, smem, vmem, vmem, hbm, hbm],
-        out_specs=(vmem, vmem),
+        out_specs=(hbm, hbm),
         scratch_shapes=[
             pltpu.VMEM((2, 4, 4) + block, BF16),
             pltpu.VMEM((2, BROWS, HALF), BF16),
@@ -446,6 +492,8 @@
             pltpu.VMEM((2, 8) + block, BF16),
             pltpu.VMEM((2, 2) + block, BF16),
             pltpu.VMEM((4, ROWS, 128), F32),
+            pltpu.VMEM((2, 2) + block, F32),
+            pltpu.SemaphoreType.DMA((2, 2)),
             pltpu.SemaphoreType.DMA((4,)),
             pltpu.SemaphoreType.DMA((count,)),
             pltpu.SemaphoreType.DMA((count,)),
@@ -454,6 +502,18 @@
             collective_id=0, has_side_effects=True, vmem_limit_bytes=66 * 1000 * 1000
         ),
     )(occ_alpha, occ_beta, virt_alpha.reshape(12, 128), virt_beta.reshape(12, 128), orbital_alpha, orbital_beta)
+    return pl.pallas_call(
+        hand_over,
+        out_shape=(out, out),
+        in_specs=[hbm, hbm],
+        out_specs=(hbm, hbm),
+        scratch_shapes=[
+            pltpu.VMEM((2, 2) + block, F32),
+            pltpu.SemaphoreType.DMA((2, 2)),
+            pltpu.SemaphoreType.DMA((2, 2)),
+        ],
+        compiler_params=pltpu.CompilerParams(vmem_limit_bytes=66 * 1000 * 1000),
+    )(*sums)
 
 
 def solution(mesh):

time: 72.6 us -> 71 us (0.978)
  local copies, waits for them, and re-layouts: 2.68 us -> 0 us
  Pallas kernels: 68.8 us -> 70 us
    unnamed x4 -> x0, local copies, waits for them, and re-layouts: 2.68 us -> none
    pallas_call x0 -> x1, Pallas kernels: none -> 2.07 us  [body(): pl.pallas_call(hand_over, out_shape=(out, out), in_specs=[hbm, hbm], out_...]
    pallas_call x1, Pallas kernels: 68.8 us -> 67.9 us  [body(): pl.pallas_call(kernel, out_shape=(out, out), in_specs=[smem, smem, vmem,...]
where the time goes in v3:
time: 71 us; the launch traced here: 70.8 us
  Pallas kernels  70 us (99%)
  between operations  0.8 us (1%)
    pallas_call x1, Pallas kernels, body(): pl.pallas_call(kernel, out_shape=(out, out), in_specs=[smem, smem, vmem,...  67.9 us
    pallas_call x1, Pallas kernels, body(): pl.pallas_call(hand_over, out_shape=(out, out), in_specs=[hbm, hbm], out_...  2.07 us

profile of v3, /device:TPU:1, one launch (start us, length us, event | category | flops | bytes accessed | tf_op | source)
XLA Modules:
  0.0 70.8 jit_solution(15176741086708852729)
XLA Ops:
  0.6 67.9 %shard_map.77 = (f32[1,48,2560]{2,1,0:T(8,128)}, f32[1,48,2560]{2,1,0:T(8,128)}) custom-call(f32[8]{0:T(128)} %occ_a.1, f32[8]{0:T(128)} %occ_b.1, f32[12,128]{1,0:T(8,128)} %bitcast.2, f32[12,128]{1,0:T(8,128)} %bitcast.3, bf16[1,48,2560]{2,1,0:T(8,128)(2,1)} %a_hbm.1, bf16[1,48,2560]{2,1,0:T(8,128)(2,1)} %b_hbm.1), custom_call_target="tpu_custom_call" | custom-call | tf_op jit(solution)/shard_map/pallas_call | solution.py:470
  68.5 2.1 %shard_map.78 = (f32[1,48,2560]{2,1,0:T(8,128)}, f32[1,48,2560]{2,1,0:T(8,128)}) custom-call(f32[1,48,2560]{2,1,0:T(8,128)} %get-tuple-element.4.ga_in, f32[1,48,2560]{2,1,0:T(8,128)} %get-tuple-element.5.gb_in), custom_call_target="tpu_custom_call" | custom-call | tf_op jit(solution)/shard_map/pallas_call | solution.py:505

commit v4 on v3

v4 whole, which is shorter than its diff:
```python
import functools

import jax
import jax.numpy as jnp
from jax import lax
from jax.experimental import pallas as pl
from jax.experimental.pallas import tpu as pltpu
from jax.sharding import PartitionSpec as P

MESH = pl.DeviceIdType.MESH
ROWS = 48
HALF = 1280
QUART = 640
BROWS = 768
POS = {0: 0, 1: 1, 7: 2, 2: 3, 6: 4, 3: 5, 5: 6, 4: 7}
SCALE = 2.0**41
TINY = 1e-37
F32 = jnp.float32
BF16 = jnp.bfloat16


def kernel(
    occ_a, occ_b, virt_a, virt_b, a_hbm, b_hbm, ga_out, gb_out,
    A, B, I, T, TT, G, GBO, GBS, GBR, S1, R1A, R1B, S2, R2A, R2B, SZ, RZ, RZ0, VA, RD,
    OUT, out_sem, local_sem, send_sem, recv_sem,
):
    grp = lax.axis_index("grp")
    slab = lax.axis_index("slab")
    z_hi, y = grp // 4, grp % 4
    x, z_lo, core = slab // 8, (slab // 2) % 4, slab % 2
    z = z_hi * 4 + z_lo

    def device(dx=0, dy=0, dz=0, dc=0):
        nx, ny, nz, nc = (x + dx) % 4, (y + dy) % 4, (z + dz) % 8, (core + dc) % 2
        return ((nz // 4) * 4 + ny, nx * 8 + (nz % 4) * 2 + nc)

    xy = {(0, 1): device(dx=1), (0, -1): device(dx=3), (1, 1): device(dy=1), (1, -1): device(dy=3)}
    zdev = {1: device(dz=1), -1: device(dz=7)}
    sibling = device(dc=1)

    local = []
    for h in range(2):
        cols = pl.ds(h * HALF, HALF)
        local.append(pltpu.make_async_copy(a_hbm.at[0, :, cols], A.at[h, 0, 0], local_sem.at[h]))
        local.append(pltpu.make_async_copy(b_hbm.at[0, :, cols], B.at[h, pl.ds(0, ROWS)], local_sem.at[2 + h]))
    for copy in local:
        copy.start()

    barrier = pltpu.get_barrier_semaphore()
    for neighbour in list(xy.values()) + list(zdev.values()) + [sibling]:
        pl.semaphore_signal(barrier, inc=1, device_id=neighbour, device_id_type=MESH)

    copies = {}

    def remote(name, src, dst, dev):
        index = len(copies)
        copies[name] = pltpu.make_async_remote_copy(
            src_ref=src, dst_ref=dst, send_sem=send_sem.at[index], recv_sem=recv_sem.at[index],
            device_id=dev, device_id_type=MESH,
        )

    def start(*names):
        for name in names:
            copies[name].start()

    def arrived(*names):
        for name in names:
            copies[name].wait_recv()

    def ablock(h, d1, d2):
        return A.at[0, d2, d1] if h == 0 else A.at[1, d1, d2]

    def bblock(h, r, k=0):
        return B.at[h, pl.ds(POS[r % 8] * 96 + k * ROWS, ROWS)]

    first, second = pl.ds(0, QUART), pl.ds(QUART, QUART)
    for h in range(2):
        one, two = h, 1 - h
        remote(("p1+", h), ablock(h, 0, 0), ablock(h, 3, 0), xy[one, 1])
        remote(("p1-", h), ablock(h, 0, 0), ablock(h, 1, 0), xy[one, -1])
        remote(("p1f+", h), ablock(h, 3, 0).at[:, first], ablock(h, 2, 0).at[:, first], xy[one, 1])
        remote(("p1f-", h), ablock(h, 1, 0).at[:, second], ablock(h, 2, 0).at[:, second], xy[one, -1])
        for u in range(4):
            remote(("p2+", h, u), ablock(h, u, 0), ablock(h, u, 3), xy[two, 1])
            remote(("p2-", h, u), ablock(h, u, 0), ablock(h, u, 1), xy[two, -1])
            if u % 2 == 0:
                remote(("p2f", h, u), ablock(h, u, 3), ablock(h, u, 2), xy[two, 1])
            else:
                remote(("p2f", h, u), ablock(h, u, 1), ablock(h, u, 2), xy[two, -1])
        for r in range(8):
            remote(("sib", h, r), bblock(h, r, 0), bblock(h, r, 1), sibling)

        for u in range(4):
            remote(("1a", h, u), S1.at[h, 2, u], R1A.at[h, u], xy[two, 1 if u % 2 == 0 else -1])
            remote(("1b+", h, u), S1.at[h, 1, u], R1B.at[h, 0, u], xy[two, 1])
            remote(("1b-", h, u), S1.at[h, 3, u], R1B.at[h, 1, u], xy[two, -1])
        remote(("2a+", h), S2.at[h, 2, :, first], R2A.at[h, :, first], xy[one, 1])
        remote(("2a-", h), S2.at[h, 2, :, second], R2A.at[h, :, second], xy[one, -1])
        remote(("2b+", h), S2.at[h, 1], R2B.at[h, 0], xy[one, 1])
        remote(("2b-", h), S2.at[h, 3], R2B.at[h, 1], xy[one, -1])
        for p in range(8):
            remote(("gsib", h, p), GBS.at[h, p], GBR.at[h, p], sibling)

    for q in range(4):
        h, cols = q // 2, (first, second)[q % 2]

        def bquarter(r):
            return bblock(h, r).at[:, cols]

        for k in range(1, 4):
            remote(("z+", q, k), bquarter(1 - k), bquarter(-k), zdev[1])
            remote(("z-", q, k), bquarter(k - 1), bquarter(k), zdev[-1])
        if h == 0:
            remote(("z4", q), bquarter(5), bquarter(4), zdev[1])
            remote(("rz", q, 4), SZ.at[q, 4], RZ.at[q, 3], zdev[1])
        else:
            remote(("z4", q), bquarter(3), bquarter(4), zdev[-1])
            remote(("rz", q, 4), SZ.at[q, 4], RZ.at[q, 5], zdev[-1])
        for r in (3, 2):
            remote(("rz", q, r), SZ.at[q, r], RZ.at[q, r - 1], zdev[1])
            remote(("rz", q, 8 - r), SZ.at[q, 8 - r], RZ.at[q, 9 - r], zdev[-1])
        remote(("rz", q, 1), SZ.at[q, 1], RZ0.at[q, 0], zdev[1])
        remote(("rz", q, 7), SZ.at[q, 7], RZ0.at[q, 1], zdev[-1])

    def encode(value):
        scaled = value * SCALE
        return (scaled * jnp.abs(scaled)).astype(BF16)

    def decode(code):
        wide = code.astype(F32)
        return wide * lax.rsqrt(jnp.maximum(jnp.abs(wide), TINY)) * (1.0 / SCALE)

    def integrals(h, d2, low, width):
        left = (A[0, d2] if h == 0 else A[1, :, d2]).reshape(4 * ROWS, HALF)
        right = B[h, pl.ds(low, width), :]
        value = lax.dot_general(left, right, (((1,), (1,)), ((), ())), preferred_element_type=F32)
        value = value.reshape(4, ROWS, width)
        if h == 0:
            I[0, d2, :, :, pl.ds(low, width)] = value
        else:
            I[1, :, d2, :, pl.ds(low, width)] = value

    def ratio(number, dy, dx, tile):
        return (number * RD[dy, dx, :, pl.ds(tile * 128, 128)]).astype(BF16)

    def transpose(tile):
        square = T[:, :, :, pl.ds(tile * 128, 128)].reshape(BROWS, 128)
        TT[pl.ds(tile * 128, 128), :] = jnp.transpose(square.astype(F32)).astype(BF16)

    def amplitudes(count, place):
        def one(block, carry):
            dy, dx = place(block)
            for tile in range(5):
                at = pl.ds(tile * 128, 128)
                T[dy, dx, :, at] = ratio(I[0, dy, dx, :, at] + I[1, dy, dx, :, at], dy, dx, tile)
            return carry

        lax.fori_loop(0, count, one, 0)

    def near(index):
        return index + index // 2

    def near_place(block):
        return near(block // 3), near(block % 3)

    def far_place(block):
        row = block < 4
        return jnp.where(row, 2, near(block - 4)), jnp.where(row, block, 2)

    def last_amplitudes(dy):
        at = pl.ds(640, 128)
        value = None
        for h in range(2):
            left = A[h, dy].reshape(4 * ROWS, HALF)
            term = lax.dot_general(left, B[h, at, :], (((1,), (1,)), ((), ())), preferred_element_type=F32)
            value = term if value is None else value + term
        for dx in range(4):
            T[dy, dx, :, at] = ratio(value[dx * ROWS:(dx + 1) * ROWS], dy, dx, 5)

    def alpha_term(h, d2):
        raw = {2: (0, 1, 2, 3), 1: (1, 3), 3: (0, 2), 0: ()}[d2]

        def one(j, carry):
            at = pl.ds(pl.multiple_of(j * 256, 256), 256)
            left = (T[d2] if h == 0 else T[:, d2]).reshape(4 * ROWS, BROWS)
            value = jnp.dot(left, B[h, :, at], preferred_element_type=F32)
            for u in range(4):
                block = value[u * ROWS:(u + 1) * ROWS]
                if u in raw:
                    S1[h, d2, u, :, at] = encode(block)
                else:
                    G[h, d2, u, :, at] = block
            return carry

        lax.fori_loop(0, 5, one, 0, unroll=True)

    def beta_term(h, low, high):
        def one(j, carry):
            at = pl.ds(pl.multiple_of(j * 256, 256), 256)
            right = A[h, :, :, :, at].reshape(BROWS, 256)
            value = jnp.dot(TT[pl.ds(low * 96, (high - low) * 96), :], right, preferred_element_type=F32)
            for p in range(low, high):
                base = (p - low) * 96
                GBO[h, p, :, at] = value[base:base + ROWS]
                GBS[h, p, :, at] = value[base + ROWS:base + 2 * ROWS]
            return carry

        lax.fori_loop(0, 5, one, 0, unroll=True)
        for p in range(low, high):
            start(("gsib", h, p))

    def by_rows(body):
        def one(step, carry):
            body(pl.ds(pl.multiple_of(step * 16, 16), 16))
            return carry

        lax.fori_loop(0, ROWS // 16, one, 0)

    for copy in local:
        copy.wait()
    pl.semaphore_wait(barrier, 7)
    H = (0, 1)
    def z_pass(k, q):
        h = q // 2
        arrived(("z+", q, k), ("z-", q, k))
        if k < 3:
            start(("z+", q, k + 1), ("z-", q, k + 1))
        else:
            start(("z4", q))
        if q % 2 == 1:
            start(("sib", h, k), ("sib", h, 8 - k))

    for h in H:
        start(("p1+", h), ("p1-", h))
    for q in range(4):
        start(("z+", q, 1), ("z-", q, 1))
    for h in H:
        start(("p2+", h, 0), ("p2-", h, 0))
    for h in H:
        start(("sib", h, 0))

    eye = lax.broadcasted_iota(jnp.int32, (ROWS, 128), 0) == lax.broadcasted_iota(jnp.int32, (ROWS, 128), 1)

    def energies(ref, column):
        return jnp.concatenate([ref[pl.ds(3 * column + i, 1), :] for i in range(3)], axis=1)

    for dx in range(4):
        row = jnp.broadcast_to(energies(virt_a, (x + dx) % 4), (8, 384))
        row = pltpu.roll(row, (384 - 96 * z_lo - 48 * core) % 384, 1)[0:1, :128]
        column = jnp.sum(jnp.where(eye, jnp.broadcast_to(row, (ROWS, 128)), 0.0), axis=1, keepdims=True)
        VA[dx] = jnp.broadcast_to(column, (ROWS, 128))
    lanes = lax.broadcasted_iota(jnp.int32, (8, BROWS), 1)
    part = energies(virt_b, x)
    ring_virt = jnp.broadcast_to(jnp.concatenate([part, part], axis=1), (8, BROWS))
    ring_occ = jnp.where(lanes < 384, occ_b[y], occ_b[4 + y])
    vb = jnp.zeros((8, BROWS), F32)
    ob = jnp.zeros((8, BROWS), F32)
    for r, p in POS.items():
        there = (z + r) % 8
        for k in range(2):
            shift = (96 * p + 768 - 96 * there + (48 * core if k else 768 - 48 * core)) % 768
            here = (lanes >= 96 * p + 48 * k) & (lanes < 96 * p + 48 * k + 48)
            vb = jnp.where(here, pltpu.roll(ring_virt, shift, 1), vb)
            ob = jnp.where(here, pltpu.roll(ring_occ, shift, 1), ob)
    vb, ob = vb[0:1], ob[0:1]

    def inverses(block, carry):
        dy, dx = block // 4, block % 4
        occ = occ_a[z_hi * 4 + (y + dy) % 4]
        for tile in range(6):
            lanes = slice(tile * 128, tile * 128 + 128)
            RD[dy, dx, :, pl.ds(tile * 128, 128)] = -1.0 / (VA[dx] + vb[:, lanes] - occ - ob[:, lanes])
        return carry

    lax.fori_loop(0, 16, inverses, 0)

    z_pass(1, 0)
    for h in H:
        arrived(("p1+", h), ("p1-", h))
        start(("p1f+", h), ("p1f-", h))
    for u in (3, 1):
        for h in H:
            start(("p2+", h, u), ("p2-", h, u))
    z_pass(1, 1)
    z_pass(1, 2)
    z_pass(1, 3)
    z_pass(2, 0)
    for h in H:
        arrived(("p1f+", h), ("p1f-", h))
        start(("p2+", h, 2), ("p2-", h, 2))
    for h in H:
        arrived(("p2+", h, 0), ("p2-", h, 0))
        start(("p2f", h, 0))
    z_pass(2, 1)
    for h in H:
        arrived(("sib", h, 0), ("sib", h, 1), ("sib", h, 7))
        integrals(h, 0, 0, 256)
    z_pass(2, 2)
    for h in H:
        arrived(("p2+", h, 3), ("p2-", h, 3))
        start(("p2f", h, 3))
    z_pass(2, 3)
    z_pass(3, 0)
    for h in H:
        arrived(("p2+", h, 1), ("p2-", h, 1))
        start(("p2f", h, 1))
    z_pass(3, 1)
    z_pass(3, 2)
    for h in H:
        arrived(("p2+", h, 2), ("p2-", h, 2))
        start(("p2f", h, 2))
    z_pass(3, 3)
    for h in H:
        integrals(h, 1, 0, 256)
        integrals(h, 3, 0, 256)
    for h in H:
        arrived(("sib", h, 2), ("sib", h, 6), ("sib", h, 3))
        for d2 in (0, 1, 3):
            integrals(h, d2, 256, 256)
    for h in H:
        arrived(("z4", 2 * h), ("z4", 2 * h + 1))
        start(("sib", h, 4))
    for h in H:
        arrived(("sib", h, 5))
        for d2 in (0, 1, 3):
            integrals(h, d2, 512, 128)
    amplitudes(9, near_place)
    for h in H:
        for u in (0, 3, 1, 2):
            arrived(("p2f", h, u))
        integrals(h, 2, 0, 256)
        integrals(h, 2, 256, 256)
        integrals(h, 2, 512, 128)
    for h in H:
        arrived(("sib", h, 4))
    for dy in range(4):
        last_amplitudes(dy)
    transpose(5)

    outward = {}

    def put(which, h):
        target = (ga_out, gb_out)[which].at[0, :, pl.ds(h * HALF, HALF)]
        outward[which, h] = pltpu.make_async_copy(OUT.at[which, h], target, out_sem.at[which, h])
        outward[which, h].start()

    def add_first(h, u):
        d2 = 1 if u % 2 == 0 else 3
        arrived(("1a", h, u))

        def body(rows):
            S1[h, d2, u, rows] = encode(G[h, d2, u, rows] + decode(R1A[h, u, rows]))

        by_rows(body)
        start(("1b+" if d2 == 1 else "1b-", h, u))

    def plane_sum(h, u, rows):
        return G[h, 0, u, rows] + decode(R1B[h, 0, u, rows]) + decode(R1B[h, 1, u, rows])

    def z_send(q, r):
        h, p, cols = q // 2, POS[r], (first, second)[q % 2]
        chained = r in (1, 2, 6, 7) or (r, h) in ((3, 0), (5, 1))
        if q % 2 == 0:
            arrived(("gsib", h, p))
        if (r, h) in ((3, 0), (5, 1)):
            arrived(("rz", q, 4))
        elif chained:
            arrived(("rz", q, r + 1 if r < 4 else r - 1))

        def body(rows):
            value = GBO[h, p, rows, cols] + GBR[h, p, rows, cols]
            if chained:
                value = value + decode(RZ[q, r, rows])
            SZ[q, r, rows] = encode(value)

        by_rows(body)
        start(("rz", q, r))

    steps = [((0, 4), (2, 4)), ((1, 4), (3, 4)), ((2, 3), (0, 5)), ((3, 3), (1, 5))]
    for r in (3, 2, 1):
        steps += [((0, r), (2, 8 - r)), ((1, r), (3, 8 - r))]
        if r > 1:
            steps += [((2, r - 1), (0, 9 - r)), ((3, r - 1), (1, 9 - r))]

    def z_step(index):
        for q, r in steps[index]:
            z_send(q, r)

    def second_far(h):
        arrived(("1b+", h, 2), ("1b-", h, 2))

        def body(rows):
            S2[h, 2, rows] = encode(plane_sum(h, 2, rows))

        by_rows(body)
        start(("2a+", h), ("2a-", h))

    def second_near(h, u):
        arrived(("1b+", h, u), ("1b-", h, u))
        arrived(("2a+" if u == 1 else "2a-", h))
        added, plain = (first, second) if u == 1 else (second, first)

        def body(rows):
            value = plane_sum(h, u, rows)
            S2[h, u, rows, plain] = encode(value[:, :QUART] if u == 3 else value[:, QUART:])
            value = value[:, QUART:] if u == 3 else value[:, :QUART]
            S2[h, u, rows, added] = encode(value + decode(R2A[h, rows, added]))

        by_rows(body)
        start(("2b+" if u == 1 else "2b-", h))

    for h in H:
        beta_term(h, 7, 8)
    amplitudes(7, far_place)
    for tile in range(5):
        transpose(tile)
    for h in H:
        alpha_term(h, 2)
        for u in (2, 1, 3, 0):
            start(("1a", h, u))
        if h == 0:
            z_step(0)
    beta_term(1, 5, 7)
    z_step(1)
    beta_term(0, 5, 7)
    for h in H:
        alpha_term(h, 3)
        start(("1b-", h, 2))
    z_step(2)
    alpha_term(0, 1)
    z_step(3)
    alpha_term(1, 1)
    beta_term(1, 3, 5)
    z_step(4)
    for h in H:
        add_first(h, 2)
        start(("1b+", h, 1))
    z_step(5)
    for h in H:
        add_first(h, 1)
    beta_term(0, 3, 5)
    z_step(6)
    for h in H:
        start(("1b+", h, 3))
        add_first(h, 3)
    z_step(7)
    for h in H:
        alpha_term(h, 0)
    beta_term(1, 1, 3)
    z_step(8)
    beta_term(0, 1, 3)
    for h in H:
        second_far(h)
    for h in H:
        start(("1b-", h, 0))
        add_first(h, 0)
    z_step(9)
    z_step(10)
    for h in H:
        beta_term(h, 0, 1)
    z_step(11)
    z_step(12)
    for h in H:
        second_near(h, 1)
        second_near(h, 3)
    z_step(13)
    for h in H:
        arrived(("1b+", h, 0), ("1b-", h, 0))

        def body(rows):
            G[h, 0, 0, rows] = plane_sum(h, 0, rows)

        by_rows(body)
    for h in H:
        arrived(("gsib", h, 0))
        for q in (2 * h, 2 * h + 1):
            arrived(("rz", q, 1), ("rz", q, 7))

        def body(rows):
            for part, cols in enumerate((first, second)):
                q = 2 * h + part
                OUT[1, h, rows, cols] = (
                    GBO[h, 0, rows, cols] + GBR[h, 0, rows, cols] + decode(RZ0[q, 0, rows]) + decode(RZ0[q, 1, rows])
                )

        by_rows(body)
        put(1, h)
    for h in H:
        arrived(("2b+", h), ("2b-", h))

        def body(rows):
            OUT[0, h, rows] = (
                G[h, 0, 0, rows] + decode(R2B[h, 0, rows]) + decode(R2B[h, 1, rows])
            )

        by_rows(body)
        put(0, h)
    for copy in list(outward.values()):
        copy.wait()
    for copy in copies.values():
        copy.wait_send()


def hand_over(ga_in, gb_in, ga_out, gb_out, held, in_sem, out_sem):
    pairs = [(w, h) for h in range(2) for w in range(2)]
    source, target = (ga_in, gb_in), (ga_out, gb_out)
    inward = [
        pltpu.make_async_copy(source[w].at[0, :, pl.ds(h * HALF, HALF)], held.at[w, h], in_sem.at[w, h])
        for w, h in pairs
    ]
    outward = [
        pltpu.make_async_copy(held.at[w, h], target[w].at[0, :, pl.ds(h * HALF, HALF)], out_sem.at[w, h])
        for w, h in pairs
    ]
    for copy in inward:
        copy.start()
    for before, after in zip(inward, outward):
        before.wait()
        after.start()
    for copy in outward:
        copy.wait()


def body(orbital_alpha, orbital_beta, occ_alpha, occ_beta, virt_alpha, virt_beta):
    block = (ROWS, HALF)
    smem = pl.BlockSpec(memory_space=pltpu.SMEM)
    vmem = pl.BlockSpec(memory_space=pltpu.VMEM)
    hbm = pl.BlockSpec(memory_space=pl.ANY)
    out = jax.ShapeDtypeStruct((1, ROWS, 2 * HALF), F32)
    count = 160
    sums = pl.pallas_call(
        kernel,
        out_shape=(out, out),
        in_specs=[smem, smem, vmem, vmem, hbm, hbm],
        out_specs=(hbm, hbm),
        scratch_shapes=[
            pltpu.VMEM((2, 4, 4) + block, BF16),
            pltpu.VMEM((2, BROWS, HALF), BF16),
            pltpu.VMEM((2, 4, 4, ROWS, BROWS), F32),
            pltpu.VMEM((4, 4, ROWS, BROWS), BF16),
            pltpu.VMEM((BROWS, BROWS), BF16),
            pltpu.VMEM((2, 4, 4) + block, F32),
            pltpu.VMEM((2, 8) + block, F32),
            pltpu.VMEM((2, 8) + block, F32),
            pltpu.VMEM((2, 8) + block, F32),
            pltpu.VMEM((2, 4, 4) + block, BF16),
            pltpu.VMEM((2, 4) + block, BF16),
            pltpu.VMEM((2, 2, 4) + block, BF16),
            pltpu.VMEM((2, 4) + block, BF16),
            pltpu.VMEM((2,) + block, BF16),
            pltpu.VMEM((2, 2) + block, BF16),
            pltpu.VMEM((4, 8, ROWS, QUART), BF16),
            pltpu.VMEM((4, 8, ROWS, QUART), BF16),
            pltpu.VMEM((4, 2, ROWS, QUART), BF16),
            pltpu.VMEM((4, ROWS, 128), F32),
            pltpu.VMEM((4, 4, ROWS, BROWS), F32),
            pltpu.VMEM((2, 2) + block, F32),
            pltpu.SemaphoreType.DMA((2, 2)),
            pltpu.SemaphoreType.DMA((4,)),
            pltpu.SemaphoreType.DMA((count,)),
            pltpu.SemaphoreType.DMA((count,)),
        ],
        compiler_params=pltpu.CompilerParams(
            collective_id=0, has_side_effects=True, vmem_limit_bytes=66 * 1000 * 1000
        ),
    )(occ_alpha, occ_beta, virt_alpha.reshape(12, 128), virt_beta.reshape(12, 128), orbital_alpha, orbital_beta)
    return pl.pallas_call(
        hand_over,
        out_shape=(out, out),
        in_specs=[hbm, hbm],
        out_specs=(hbm, hbm),
        scratch_shapes=[
            pltpu.VMEM((2, 2) + block, F32),
            pltpu.SemaphoreType.DMA((2, 2)),
            pltpu.SemaphoreType.DMA((2, 2)),
        ],
        compiler_params=pltpu.CompilerParams(vmem_limit_bytes=66 * 1000 * 1000),
    )(*sums)


def solution(mesh):
    in_specs = (P("grp", "slab", None), P("grp", "slab", None), P(), P(), P(), P())
    out_specs = (P("grp", "slab", None), P("grp", "slab", None))
    return jax.shard_map(body, mesh=mesh, in_specs=in_specs, out_specs=out_specs, check_vma=False)
```

time: 71 us -> 69.1 us (0.973)
  Pallas kernels: 70 us -> 68.3 us
    pallas_call x1, Pallas kernels: 67.9 us -> 66.2 us  [body(): pl.pallas_call(kernel, out_shape=(out, out), in_specs=[smem, smem, vmem,...]
where the time goes in v4:
time: 69.1 us; the launch traced here: 69 us
  Pallas kernels  68.3 us (99%)
    pallas_call x1, Pallas kernels, body(): pl.pallas_call(kernel, out_shape=(out, out), in_specs=[smem, smem, vmem,...  66.2 us
    pallas_call x1, Pallas kernels, body(): pl.pallas_call(hand_over, out_shape=(out, out), in_specs=[hbm, hbm], out_...  2.07 us

profile of v4, /device:TPU:1, one launch (start us, length us, event | category | flops | bytes accessed | tf_op | source)
XLA Modules:
  0.0 69.0 jit_solution(13808475422512204346)
XLA Ops:
  0.6 66.2 %shard_map.77 = (f32[1,48,2560]{2,1,0:T(8,128)}, f32[1,48,2560]{2,1,0:T(8,128)}) custom-call(f32[8]{0:T(128)} %occ_a.1, f32[8]{0:T(128)} %occ_b.1, f32[12,128]{1,0:T(8,128)} %bitcast.2, f32[12,128]{1,0:T(8,128)} %bitcast.3, bf16[1,48,2560]{2,1,0:T(8,128)(2,1)} %a_hbm.1, bf16[1,48,2560]{2,1,0:T(8,128)(2,1)} %b_hbm.1), custom_call_target="tpu_custom_call" | custom-call | tf_op jit(solution)/shard_map/pallas_call | solution.py:531
  66.9 2.1 %shard_map.78 = (f32[1,48,2560]{2,1,0:T(8,128)}, f32[1,48,2560]{2,1,0:T(8,128)}) custom-call(f32[1,48,2560]{2,1,0:T(8,128)} %get-tuple-element.4.ga_in, f32[1,48,2560]{2,1,0:T(8,128)} %get-tuple-element.5.gb_in), custom_call_target="tpu_custom_call" | custom-call | tf_op jit(solution)/shard_map/pallas_call | solution.py:567

commit v5 on v4

--- a/solution.py
+++ b/solution.py
@@ -427,11 +427,11 @@
         alpha_term(h, 3)
         start(("1b-", h, 2))
     z_step(2)
+    z_step(3)
     alpha_term(0, 1)
-    z_step(3)
     alpha_term(1, 1)
+    z_step(4)
     beta_term(1, 3, 5)
-    z_step(4)
     for h in H:
         add_first(h, 2)
         start(("1b+", h, 1))
@@ -460,10 +460,10 @@
         beta_term(h, 0, 1)
     z_step(11)
     z_step(12)
+    z_step(13)
     for h in H:
         second_near(h, 1)
         second_near(h, 3)
-    z_step(13)
     for h in H:
         arrived(("1b+", h, 0), ("1b-", h, 0))
 

time: 69.1 us -> 68.8 us (level)
  no operation moved by 1% of the time
where the time goes in v5:
time: 68.8 us; the launch traced here: 68.6 us
  Pallas kernels  68 us (99%)
    pallas_call x1, Pallas kernels, body(): pl.pallas_call(kernel, out_shape=(out, out), in_specs=[smem, smem, vmem,...  65.9 us
    pallas_call x1, Pallas kernels, body(): pl.pallas_call(hand_over, out_shape=(out, out), in_specs=[hbm, hbm], out_...  2.07 us

profile of v5, /device:TPU:1, one launch (start us, length us, event | category | flops | bytes accessed | tf_op | source)
XLA Modules:
  0.0 68.6 jit_solution(17878618129524688559)
XLA Ops:
  0.6 65.9 %shard_map.77 = (f32[1,48,2560]{2,1,0:T(8,128)}, f32[1,48,2560]{2,1,0:T(8,128)}) custom-call(f32[8]{0:T(128)} %occ_a.1, f32[8]{0:T(128)} %occ_b.1, f32[12,128]{1,0:T(8,128)} %bitcast.2, f32[12,128]{1,0:T(8,128)} %bitcast.3, bf16[1,48,2560]{2,1,0:T(8,128)(2,1)} %a_hbm.1, bf16[1,48,2560]{2,1,0:T(8,128)(2,1)} %b_hbm.1), custom_call_target="tpu_custom_call" | custom-call | tf_op jit(solution)/shard_map/pallas_call | solution.py:531
  66.6 2.1 %shard_map.78 = (f32[1,48,2560]{2,1,0:T(8,128)}, f32[1,48,2560]{2,1,0:T(8,128)}) custom-call(f32[1,48,2560]{2,1,0:T(8,128)} %get-tuple-element.4.ga_in, f32[1,48,2560]{2,1,0:T(8,128)} %get-tuple-element.5.gb_in), custom_call_target="tpu_custom_call" | custom-call | tf_op jit(solution)/shard_map/pallas_call | solution.py:567
